TPU v7x, 32 devices: a whole 2x2x4 slice. The times are simulated.
32 devices in a mesh: dp: 8 (over y, x, core), tensor: 4 (over z).
Axes of the slice: x: 2, y: 2, z: 4, core: 2. Of those that a mesh axis runs over, the one named last changes fastest.
Arguments:
- inputs: bfloat16 [8, 1024, 2048], P('dp', 'tensor'), may hold values from -6 to 6
- teacher: bfloat16 [8, 1024, 2048], P('dp', 'tensor'), may hold values from -6 to 6
- lengths: int32 [8], P('dp'), may hold values from 1 to 1024, 5120 in all
- w_query: bfloat16 [2048, 2048], P('dp', 'tensor'), may hold values from -0.1875 to 0.1875
- w_key: bfloat16 [2048, 2048], P('dp', 'tensor'), may hold values from -0.1875 to 0.1875
- w_value: bfloat16 [2048, 2048], P('dp', 'tensor'), may hold values from -0.125 to 0.125
- w_out: bfloat16 [2048, 2048], P('tensor', 'dp'), may hold values from -2 to 2
- w_gate: bfloat16 [2048, 8192], P('dp', 'tensor'), may hold values from -0.125 to 0.125
- w_up: bfloat16 [2048, 8192], P('dp', 'tensor'), may hold values from -0.125 to 0.125
- w_down: bfloat16 [8192, 2048], P('tensor', 'dp'), may hold values from -0.0625 to 0.0625
Outputs:
- output: bfloat16 [8, 1024, 2048], P('dp', 'tensor')
- loss: float32 [], replicated
- grad_input: float32 [8, 1024, 2048], P('dp', 'tensor')
- grad_query: float32 [2048, 2048], P('dp', 'tensor')
- grad_key: float32 [2048, 2048], P('dp', 'tensor')
- grad_value: float32 [2048, 2048], P('dp', 'tensor')
- grad_out: float32 [2048, 2048], P('tensor', 'dp')
- grad_gate: float32 [2048, 8192], P('dp', 'tensor')
- grad_up: float32 [2048, 8192], P('dp', 'tensor')
- grad_down: float32 [8192, 2048], P('tensor', 'dp')
Inputs may be any that keep to these rules, and one draw needn't show every extreme that they name: Sequence s holds lengths[s] valid tokens at its start; its other slots of 1024 are padding; some sequence fills all 1024 slots and the lengths add up to 5120.
All inputs are finite; a program needn't handle non-finite values. No bound on the sum of `lengths` on one device may be relied on, other than what follows from the above.
Results may differ from a plain program's by a relative error of at most 0.015.
The roundings to bfloat16 on the way count: a program that leaves them out, or rounds other values in their place, can miss the bound.
Values may be sent and summed in bfloat16 or wider, within the bound.
No kernel may reach another device: no remote copies, remote signals or barrier semaphores. Data moves between devices by JAX's collectives and lax.ppermute only.
A program may use at most 192 MiB of HBM per device.

v0:
```python
import math
import jax
import jax.numpy as jnp
from jax import lax
from jax.sharding import PartitionSpec as P

HS = 128
EPSILON = 1e-05


def layer_norm(values):
    centre = values - jnp.mean(values, axis=-1, keepdims=True)
    spread = jnp.mean(centre * centre, axis=-1, keepdims=True)
    return centre * lax.rsqrt(spread + EPSILON)


def norm_back(values, grad_in):
    centre = values - jnp.mean(values, axis=-1, keepdims=True)
    spread = jnp.mean(centre * centre, axis=-1, keepdims=True)
    inverse = lax.rsqrt(spread + EPSILON)
    normed = centre * inverse
    return inverse * (
        grad_in
        - jnp.mean(grad_in, axis=-1, keepdims=True)
        - normed * jnp.mean(grad_in * normed, axis=-1, keepdims=True)
    )


def rotary_tables(length, size):
    half_size = size // 2
    inverse = jnp.exp(jnp.arange(half_size, dtype=jnp.float32) * (-2.0 * math.log(10000.0) / size))
    angles = jnp.arange(length, dtype=jnp.float32)[:, None] * inverse[None, :]
    return (jnp.cos(angles), jnp.sin(angles))


def rotate(values, cosine_table, sine_table):
    half_size = values.shape[-1] // 2
    first_half = values[..., :half_size]
    second_half = values[..., half_size:]
    cosine_rows = cosine_table[:, None, :]
    sine_rows = sine_table[:, None, :]
    return jnp.concatenate(
        [
            first_half * cosine_rows - second_half * sine_rows,
            second_half * cosine_rows + first_half * sine_rows,
        ],
        axis=-1,
    )


def rotate_back(grads, cosine_table, sine_table):
    half_size = grads.shape[-1] // 2
    first_half = grads[..., :half_size]
    second_half = grads[..., half_size:]
    cosine_rows = cosine_table[:, None, :]
    sine_rows = sine_table[:, None, :]
    return jnp.concatenate(
        [
            first_half * cosine_rows + second_half * sine_rows,
            second_half * cosine_rows - first_half * sine_rows,
        ],
        axis=-1,
    )


def local(inputs, teacher, lengths, w_query, w_key, w_value, w_out, w_gate, w_up, w_down):
    tensor_count = lax.axis_size("tensor")
    local_rows = inputs.shape[1]
    slot_count = local_rows * tensor_count
    token_total = slot_count * lax.axis_size("dp")
    width_all = inputs.shape[2]
    rows_in = inputs[0].astype(jnp.float32)
    target = teacher[0].astype(jnp.float32)
    own_length = lengths[0]
    positions = lax.axis_index("tensor") * local_rows + jnp.arange(local_rows, dtype=jnp.int32)
    valid_rows = (positions < own_length)[:, None]
    valid_total = lax.psum(own_length.astype(jnp.float32), "dp")
    gathered = (
        lax.all_gather(w_query, "dp", axis=0, tiled=True),
        lax.all_gather(w_key, "dp", axis=0, tiled=True),
        lax.all_gather(w_value, "dp", axis=0, tiled=True),
        lax.all_gather(w_gate, "dp", axis=0, tiled=True),
        lax.all_gather(w_up, "dp", axis=0, tiled=True),
        lax.all_gather(w_out, "dp", axis=1, tiled=True),
        lax.all_gather(w_down, "dp", axis=1, tiled=True),
    )
    query_full, key_full, value_full, gate_full, up_full, out_full, down_full = gathered
    head_cols = query_full.shape[1]
    head_count = head_cols // HS
    cosine_table, sine_table = rotary_tables(slot_count, HS)
    query_scale = HS ** (-0.5)
    block_rows = min(slot_count, 512)
    block_count = slot_count // block_rows
    key_index = jnp.arange(slot_count, dtype=jnp.int32)
    normed = layer_norm(rows_in).astype(jnp.bfloat16)
    features = lax.all_gather(normed, "tensor", axis=0, tiled=True)
    queries = jnp.dot(features, query_full, preferred_element_type=jnp.float32)
    key_raw = jnp.dot(features, key_full, preferred_element_type=jnp.float32)
    value_raw = jnp.dot(features, value_full, preferred_element_type=jnp.float32)
    query_rot = (
        rotate(queries.reshape(slot_count, head_count, HS), cosine_table, sine_table) * query_scale
    ).astype(jnp.bfloat16)
    key_rot = rotate(key_raw.reshape(slot_count, head_count, HS), cosine_table, sine_table).astype(
        jnp.bfloat16
    )
    value_heads = value_raw.reshape(slot_count, head_count, HS).astype(jnp.bfloat16)

    def block_scores(block):
        start = block * block_rows
        query_rows = query_rot[start : start + block_rows]
        scores = jnp.einsum("qhd,khd->hqk", query_rows, key_rot, preferred_element_type=jnp.float32)
        causal = (start + jnp.arange(block_rows, dtype=jnp.int32))[:, None] >= key_index[None, :]
        return (jnp.where(causal[None], scores, -1e30), query_rows)

    mixed_blocks = []
    lse_blocks = []
    for block in range(block_count):
        scores, query_rows = block_scores(block)
        largest = jnp.max(scores, axis=-1, keepdims=True)
        shifted = jnp.exp(scores - largest)
        totals = jnp.sum(shifted, axis=-1, keepdims=True)
        attention = shifted / totals
        lse_blocks.append(largest + jnp.log(totals))
        mixed_blocks.append(
            jnp.einsum(
                "hqk,khd->qhd",
                attention.astype(jnp.bfloat16),
                value_heads,
                preferred_element_type=jnp.float32,
            )
        )
    attended = (
        jnp.concatenate(mixed_blocks, axis=0).reshape(slot_count, head_cols).astype(jnp.bfloat16)
    )
    attn_out = lax.psum_scatter(
        jnp.dot(attended, out_full, preferred_element_type=jnp.float32),
        "tensor",
        scatter_dimension=0,
        tiled=True,
    )
    residual = rows_in + attn_out
    normed_two = layer_norm(residual).astype(jnp.bfloat16)
    features_two = lax.all_gather(normed_two, "tensor", axis=0, tiled=True)
    gate_pre = jnp.dot(features_two, gate_full, preferred_element_type=jnp.float32)
    up_pre = jnp.dot(features_two, up_full, preferred_element_type=jnp.float32)
    gate_sigmoid = jax.nn.sigmoid(gate_pre)
    activated = gate_pre * gate_sigmoid
    hidden = (activated * up_pre).astype(jnp.bfloat16)
    mlp_out = lax.psum_scatter(
        jnp.dot(hidden, down_full, preferred_element_type=jnp.float32).astype(jnp.bfloat16),
        "tensor",
        scatter_dimension=0,
        tiled=True,
    ).astype(jnp.float32)
    result = residual + mlp_out
    errors = jnp.where(valid_rows, result - target, 0.0)
    squares = jnp.sum(errors * errors)
    total_squares = lax.psum(squares, ("dp", "tensor"))
    loss_value = total_squares / (valid_total * width_all)
    grad_result = errors * (token_total / valid_total)
    regathered = (
        lax.all_gather(w_query, "dp", axis=0, tiled=True),
        lax.all_gather(w_key, "dp", axis=0, tiled=True),
        lax.all_gather(w_value, "dp", axis=0, tiled=True),
        lax.all_gather(w_gate, "dp", axis=0, tiled=True),
        lax.all_gather(w_up, "dp", axis=0, tiled=True),
        lax.all_gather(w_out, "dp", axis=1, tiled=True),
        lax.all_gather(w_down, "dp", axis=1, tiled=True),
    )
    query_full, key_full, value_full, gate_full, up_full, out_full, down_full = regathered
    down_grad_in = lax.all_gather(grad_result.astype(jnp.bfloat16), "tensor", axis=0, tiled=True)
    grad_down = jnp.einsum("tf,td->fd", hidden, down_grad_in, preferred_element_type=jnp.float32)
    hidden_grad = jnp.einsum(
        "td,fd->tf", down_grad_in, down_full, preferred_element_type=jnp.float32
    )
    gate_grad = (
        hidden_grad * up_pre * gate_sigmoid * (1.0 + gate_pre * (1.0 - gate_sigmoid))
    ).astype(jnp.bfloat16)
    up_grad = (hidden_grad * activated).astype(jnp.bfloat16)
    grad_gate = jnp.einsum("td,tf->df", features_two, gate_grad, preferred_element_type=jnp.float32)
    grad_up = jnp.einsum("td,tf->df", features_two, up_grad, preferred_element_type=jnp.float32)
    feature_grad = jnp.einsum(
        "tf,df->td", gate_grad, gate_full, preferred_element_type=jnp.float32
    ) + jnp.einsum("tf,df->td", up_grad, up_full, preferred_element_type=jnp.float32)
    normed_two_grad = lax.psum_scatter(
        feature_grad.astype(jnp.bfloat16), "tensor", scatter_dimension=0, tiled=True
    ).astype(jnp.float32)
    residual_grad = grad_result + norm_back(residual, normed_two_grad)
    attn_grad_in = lax.all_gather(residual_grad.astype(jnp.bfloat16), "tensor", axis=0, tiled=True)
    grad_out = jnp.einsum("tc,td->cd", attended, attn_grad_in, preferred_element_type=jnp.float32)
    mixed_grad = (
        jnp.einsum("td,cd->tc", attn_grad_in, out_full, preferred_element_type=jnp.float32)
        .astype(jnp.bfloat16)
        .reshape(slot_count, head_count, HS)
    )
    value_grad = jnp.zeros((slot_count, head_count, HS), jnp.float32)
    key_grad = jnp.zeros((slot_count, head_count, HS), jnp.float32)
    query_parts = []
    for block in range(block_count):
        scores, query_rows = block_scores(block)
        attention = jnp.exp(scores - lse_blocks[block])
        start = block * block_rows
        mixed_rows = mixed_grad[start : start + block_rows]
        value_grad = value_grad + jnp.einsum(
            "hqk,qhd->khd",
            attention.astype(jnp.bfloat16),
            mixed_rows,
            preferred_element_type=jnp.float32,
        )
        prob_grad = jnp.einsum(
            "qhd,khd->hqk", mixed_rows, value_heads, preferred_element_type=jnp.float32
        )
        score_grad = (
            attention * (prob_grad - jnp.sum(prob_grad * attention, axis=-1, keepdims=True))
        ).astype(jnp.bfloat16)
        query_parts.append(
            jnp.einsum("hqk,khd->qhd", score_grad, key_rot, preferred_element_type=jnp.float32)
        )
        key_grad = key_grad + jnp.einsum(
            "hqk,qhd->khd", score_grad, query_rows, preferred_element_type=jnp.float32
        )
    query_grad = (
        (rotate_back(jnp.concatenate(query_parts, axis=0), cosine_table, sine_table) * query_scale)
        .astype(jnp.bfloat16)
        .reshape(slot_count, head_cols)
    )
    key_grad_low = (
        rotate_back(key_grad, cosine_table, sine_table)
        .astype(jnp.bfloat16)
        .reshape(slot_count, head_cols)
    )
    value_grad_low = value_grad.astype(jnp.bfloat16).reshape(slot_count, head_cols)
    grad_query = jnp.einsum("td,tc->dc", features, query_grad, preferred_element_type=jnp.float32)
    grad_key = jnp.einsum("td,tc->dc", features, key_grad_low, preferred_element_type=jnp.float32)
    grad_value = jnp.einsum(
        "td,tc->dc", features, value_grad_low, preferred_element_type=jnp.float32
    )
    features_grad = (
        jnp.einsum("tc,dc->td", query_grad, query_full, preferred_element_type=jnp.float32)
        + jnp.einsum("tc,dc->td", key_grad_low, key_full, preferred_element_type=jnp.float32)
        + jnp.einsum("tc,dc->td", value_grad_low, value_full, preferred_element_type=jnp.float32)
    )
    normed_grad = lax.psum_scatter(
        features_grad.astype(jnp.bfloat16), "tensor", scatter_dimension=0, tiled=True
    ).astype(jnp.float32)
    input_grad = residual_grad + norm_back(rows_in, normed_grad)
    summed = (
        lax.psum_scatter(
            grad_query.astype(jnp.bfloat16), "dp", scatter_dimension=0, tiled=True
        ).astype(jnp.float32),
        lax.psum_scatter(
            grad_key.astype(jnp.bfloat16), "dp", scatter_dimension=0, tiled=True
        ).astype(jnp.float32),
        lax.psum_scatter(
            grad_value.astype(jnp.bfloat16), "dp", scatter_dimension=0, tiled=True
        ).astype(jnp.float32),
        lax.psum_scatter(
            grad_gate.astype(jnp.bfloat16), "dp", scatter_dimension=0, tiled=True
        ).astype(jnp.float32),
        lax.psum_scatter(
            grad_up.astype(jnp.bfloat16), "dp", scatter_dimension=0, tiled=True
        ).astype(jnp.float32),
        lax.psum_scatter(
            grad_out.astype(jnp.bfloat16), "dp", scatter_dimension=1, tiled=True
        ).astype(jnp.float32),
        lax.psum_scatter(
            grad_down.astype(jnp.bfloat16), "dp", scatter_dimension=1, tiled=True
        ).astype(jnp.float32),
    )
    return (
        result.astype(jnp.bfloat16)[None],
        loss_value,
        input_grad[None],
        summed[0],
        summed[1],
        summed[2],
        summed[5],
        summed[3],
        summed[4],
        summed[6],
    )


def solution(mesh):
    in_specs = (
        P("dp", "tensor", None),
        P("dp", "tensor", None),
        P("dp"),
        P("dp", "tensor"),
        P("dp", "tensor"),
        P("dp", "tensor"),
        P("tensor", "dp"),
        P("dp", "tensor"),
        P("dp", "tensor"),
        P("tensor", "dp"),
    )
    out_specs = (
        P("dp", "tensor", None),
        P(),
        P("dp", "tensor", None),
        P("dp", "tensor"),
        P("dp", "tensor"),
        P("dp", "tensor"),
        P("tensor", "dp"),
        P("dp", "tensor"),
        P("dp", "tensor"),
        P("tensor", "dp"),
    )
    return jax.shard_map(local, mesh=mesh, in_specs=in_specs, out_specs=out_specs, check_vma=False)
```

profile of v0, /device:TPU:0, one launch (start us, length us, event | category | flops | bytes accessed | tf_op | source)
XLA Modules:
  0.0 1495.9 jit_solution(12879193869445910565)
XLA Ops:
  19.6 21.0 %all-gather.18.cloned.1.call-done = bf16[2048,512]{1,0:T(8,128)(2,1)} async-done(((bf16[256,512]{1,0:T(8,128)(2,1)}), bf16[2048,512]{1,0:T(8,128)(2,1)}) %all-gather.18.cloned.1.call-update) | async-done | bytes 2097168 | tf_op jit(solution)/shard_map/all_gather | solution.py:80
  40.5 82.9 %all-gather.12.cloned.1.call-done = bf16[1024,2048]{1,0:T(8,128)(2,1)} async-done(((bf16[256,2048]{1,0:T(8,128)(2,1)}), bf16[1024,2048]{1,0:T(8,128)(2,1)}) %all-gather.12.cloned.1.call-update) | async-done | bytes 4194320 | tf_op jit(solution)/shard_map/all_gather | solution.py:96
  123.5 5.2 fusion.66
  135.3 16.5 %all-gather.16.cloned.1.call-done = bf16[2048,512]{1,0:T(8,128)(2,1)} async-done(((bf16[256,512]{1,0:T(8,128)(2,1)}), bf16[2048,512]{1,0:T(8,128)(2,1)}) %all-gather.16.cloned.1.call-update) | async-done | bytes 2097168 | tf_op jit(solution)/shard_map/all_gather | solution.py:79
  151.8 5.2 fusion.65
  164.9 4.3 multiply_subtract_fusion.1
  181.5 5.4 convolution_convert_fusion.9
  192.4 19.1 %all-gather.20.cloned.1.call-done = bf16[512,2048]{1,0:T(8,128)(2,1)} async-done(((bf16[512,256]{1,0:T(8,128)(2,1)}), bf16[512,2048]{1,0:T(8,128)(2,1)}) %all-gather.20.cloned.1.call-update) | async-done | bytes 2097168 | tf_op jit(solution)/shard_map/all_gather | solution.py:84
  211.5 7.2 fusion.67
  219.6 143.8 %reduce-scatter.12.cloned.1.call-done = f32[256,2048]{1,0:T(8,128)} async-done(((f32[1024,2048]{1,0:T(8,128)}), f32[256,2048]{1,0:T(8,128)}) %reduce-scatter.12.cloned.1.call-update) | async-done | bytes 2097168 | tf_op jit(solution)/shard_map/reduce_scatter | solution.py:135
  368.3 52.1 %all-gather.24.cloned.1.call-done = bf16[2048,2048]{1,0:T(8,128)(2,1)} async-done(((bf16[256,2048]{1,0:T(8,128)(2,1)}), bf16[2048,2048]{1,0:T(8,128)(2,1)}) %all-gather.24.cloned.1.call-update) | async-done | bytes 8388624 | tf_op jit(solution)/shard_map/all_gather | solution.py:82
  420.4 82.9 %all-gather.22.cloned.1.call-done = bf16[1024,2048]{1,0:T(8,128)(2,1)} async-done(((bf16[256,2048]{1,0:T(8,128)(2,1)}), bf16[1024,2048]{1,0:T(8,128)(2,1)}) %all-gather.22.cloned.1.call-update) | async-done | bytes 4194320 | tf_op jit(solution)/shard_map/all_gather | solution.py:143
  503.3 14.9 fusion.68
  518.2 40.0 %all-gather.26.cloned.1.call-done = bf16[2048,2048]{1,0:T(8,128)(2,1)} async-done(((bf16[256,2048]{1,0:T(8,128)(2,1)}), bf16[2048,2048]{1,0:T(8,128)(2,1)}) %all-gather.26.cloned.1.call-update) | async-done | bytes 8388624 | tf_op jit(solution)/shard_map/all_gather | solution.py:83
  558.2 16.9 %multiply_convert_fusion.4 = (bf16[1024,2048]{1,0:T(8,128)(2,1)}, f32[1024,2048]{1,0:T(8,128)}) fusion(f32[1024,2048]{1,0:T(8,128)} %fusion.68, bf16[1024,2048]{1,0:T(8,128)(2,1)} %all-gather.22.cloned.1.call-done, bf16[2048,2048]{1,0:T(8,128)(2,1)} %all-gather.26.cloned.1.call-done), kind=kOutput, calls=%fused_computation.10 | convolution fusion | flops 8602517504 | bytes 33554432 | tf_op jit(solution)/shard_map/dot_general | solution.py:145
  575.1 40.8 %all-gather.28.cloned.1.call-done = bf16[2048,2048]{1,0:T(8,128)(2,1)} async-done(((bf16[2048,256]{1,0:T(8,128)(2,1)}), bf16[2048,2048]{1,0:T(8,128)(2,1)}) %all-gather.28.cloned.1.call-update) | async-done | bytes 8388624 | tf_op jit(solution)/shard_map/all_gather | solution.py:85
  615.9 13.9 convolution_convert_fusion.3
  630.6 14.0 psum.15
  645.3 61.4 %reduce-scatter.14.cloned.1.call-done = bf16[256,2048]{1,0:T(8,128)(2,1)} async-done(((bf16[1024,2048]{1,0:T(8,128)(2,1)}), bf16[256,2048]{1,0:T(8,128)(2,1)}) %reduce-scatter.14.cloned.1.call-update) | async-done | bytes 1048592 | tf_op jit(solution)/shard_map/reduce_scatter | solution.py:149
  709.5 81.4 %all-gather.30.cloned.1.call-done = bf16[1024,2048]{1,0:T(8,128)(2,1)} async-done(((bf16[256,2048]{1,0:T(8,128)(2,1)}), bf16[1024,2048]{1,0:T(8,128)(2,1)}) %all-gather.30.cloned.1.call-update) | async-done | bytes 4194320 | tf_op jit(solution)/shard_map/all_gather | solution.py:171
  790.9 20.6 %multiply_convert_fusion.2 = (bf16[1024,2048]{1,0:T(8,128)(2,1)}, bf16[1024,2048]{1,0:T(8,128)(2,1)}) fusion(f32[1024,2048]{1,0:T(8,128)} %fusion.68, f32[1024,2048]{1,0:T(8,128)} %get-tuple-element.47, bf16[1024,2048]{1,0:T(8,128)(2,1)} %all-gather.30.cloned.1.call-done, bf16[2048,2048]{1,0:T(8,128)(2,1)} %all-gather.28.cloned.1.call-done), kind=kOutput, calls=%fused_computation.8 | convolution fusion | flops 8617197568 | bytes 37748736 | tf_op jit(solution)/shard_map/td,fd->tf/dot_general | solution.py:173
  811.6 12.7 fusion.69
  824.3 13.1 add_convert_fusion.1
  837.5 75.4 %reduce-scatter.16.cloned.1.call-done = bf16[256,2048]{1,0:T(8,128)(2,1)} async-done(((bf16[1024,2048]{1,0:T(8,128)(2,1)}), bf16[256,2048]{1,0:T(8,128)(2,1)}) %reduce-scatter.16.cloned.1.call-update) | async-done | bytes 1048592 | tf_op jit(solution)/shard_map/reduce_scatter | solution.py:185
  919.7 14.1 convolution_convert_fusion
  933.9 14.5 convolution_convert_fusion.1
  948.5 14.1 convolution_convert_fusion.2
  963.3 37.7 %all-gather.32.cloned.1.call-done = bf16[1024,2048]{1,0:T(8,128)(2,1)} async-done(((bf16[256,2048]{1,0:T(8,128)(2,1)}), bf16[1024,2048]{1,0:T(8,128)(2,1)}) %all-gather.32.cloned.1.call-update) | async-done | bytes 4194320 | tf_op jit(solution)/shard_map/all_gather | solution.py:189
  1001.1 4.7 convolution_convert_fusion.8
  1005.9 3.7 convolution_convert_fusion.4
  1009.9 7.0 multiply_reduce_fusion.1
  1016.9 5.3 multiply_convert_fusion.1
  1031.6 3.8 convolution_convert_fusion.5
  1035.4 7.9 multiply_reduce_fusion
  1043.6 3.8 fusion.50
  1047.4 7.1 multiply_convert_fusion
  1061.0 6.2 convolution_convert_fusion.7
  1068.6 6.3 convolution_convert_fusion.6
  1075.1 4.5 fusion.71
  1082.0 6.7 add_convert_fusion
  1089.3 39.4 %psum.14 = f32[]{:T(128)} all-reduce(f32[]{:T(128)} %get-tuple-element.11), channel_id=1, replica_groups=mesh['dp'=8,'tensor'=4] {'dp','tensor'}, use_global_device_ids=true, to_apply=%region_11.12 | all-reduce | flops 1 | bytes 8 | tf_op jit(solution)/shard_map/psum | solution.py:158
  1132.2 17.7 %reduce-scatter.30.cloned.1.call-done = bf16[256,2048]{1,0:T(8,128)(2,1)} async-done(((bf16[2048,2048]{1,0:T(8,128)(2,1)}), bf16[256,2048]{1,0:T(8,128)(2,1)}) %reduce-scatter.30.cloned.1.call-update) | async-done | bytes 1048592 | tf_op jit(solution)/shard_map/reduce_scatter | solution.py:260
  1152.6 71.8 %reduce-scatter.28.cloned.1.call-done = bf16[256,2048]{1,0:T(8,128)(2,1)} async-done(((bf16[2048,2048]{1,0:T(8,128)(2,1)}), bf16[256,2048]{1,0:T(8,128)(2,1)}) %reduce-scatter.28.cloned.1.call-update) | async-done | bytes 1048592 | tf_op jit(solution)/shard_map/reduce_scatter | solution.py:257
  1227.2 41.9 %reduce-scatter.26.cloned.1.call-done = bf16[512,256]{1,0:T(8,128)(2,1)} async-done(((bf16[512,2048]{1,0:T(8,128)(2,1)}), bf16[512,256]{1,0:T(8,128)(2,1)}) %reduce-scatter.26.cloned.1.call-update) | async-done | bytes 262160 | tf_op jit(solution)/shard_map/reduce_scatter | solution.py:263
  1270.9 42.8 %reduce-scatter.24.cloned.1.call-done = bf16[256,512]{1,0:T(8,128)(2,1)} async-done(((bf16[2048,512]{1,0:T(8,128)(2,1)}), bf16[256,512]{1,0:T(8,128)(2,1)}) %reduce-scatter.24.cloned.1.call-update) | async-done | bytes 262160 | tf_op jit(solution)/shard_map/reduce_scatter | solution.py:254
  1315.5 42.9 %reduce-scatter.20.cloned.1.call-done = bf16[256,512]{1,0:T(8,128)(2,1)} async-done(((bf16[2048,512]{1,0:T(8,128)(2,1)}), bf16[256,512]{1,0:T(8,128)(2,1)}) %reduce-scatter.20.cloned.1.call-update) | async-done | bytes 262160 | tf_op jit(solution)/shard_map/reduce_scatter | solution.py:248
  1360.3 42.8 %reduce-scatter.22.cloned.1.call-done = bf16[256,512]{1,0:T(8,128)(2,1)} async-done(((bf16[2048,512]{1,0:T(8,128)(2,1)}), bf16[256,512]{1,0:T(8,128)(2,1)}) %reduce-scatter.22.cloned.1.call-update) | async-done | bytes 262160 | tf_op jit(solution)/shard_map/reduce_scatter | solution.py:251
  1404.8 77.4 %reduce-scatter.18.cloned.1.call-done = bf16[256,2048]{1,0:T(8,128)(2,1)} async-done(((bf16[1024,2048]{1,0:T(8,128)(2,1)}), bf16[256,2048]{1,0:T(8,128)(2,1)}) %reduce-scatter.18.cloned.1.call-update) | async-done | bytes 1048592 | tf_op jit(solution)/shard_map/reduce_scatter | solution.py:243
  (217 shorter events, 101.3 us)
Async XLA Ops:
  7.2 33.4 %all-gather.18.cloned.1.call-start = ((), (), s32[]{:S(2)}) async-start(), calls=%async_computation.14 | async-start | bytes 2359296 | tf_op jit(solution)/shard_map/all_gather | solution.py:80
  7.9 115.6 %all-gather.12.cloned.1.call-start = ((), (), s32[]{:S(2)}) async-start(), calls=%async_computation.11 | async-start | bytes 5242880 | tf_op jit(solution)/shard_map/all_gather | solution.py:96
  14.2 137.6 %all-gather.16.cloned.1.call-start = ((), (), s32[]{:S(2)}) async-start(), calls=%async_computation.13 | async-start | bytes 2359296 | tf_op jit(solution)/shard_map/all_gather | solution.py:79
  14.9 166.6 %all-gather.14.cloned.1.call-start = ((), (), s32[]{:S(2)}) async-start(), calls=%async_computation.12 | async-start | bytes 2359296 | tf_op jit(solution)/shard_map/all_gather | solution.py:81
  15.5 196.0 %all-gather.20.cloned.1.call-start = ((), (), s32[]{:S(2)}) async-start(), calls=%async_computation.15 | async-start | bytes 2359296 | tf_op jit(solution)/shard_map/all_gather | solution.py:84
  16.1 347.3 %reduce-scatter.12.cloned.1.call-start = ((), (), s32[]{:S(2)}) async-start(), calls=%async_computation.16 | async-start | bytes 10485760 | tf_op jit(solution)/shard_map/reduce_scatter | solution.py:135
  16.3 173.1 %copy-start.7 = (pred[512,1024]{1,0:T(8,128)(4,1)}, pred[512,1024]{1,0:T(8,128)(4,1)S(1)}, u32[]{:S(2)}) copy-start(pred[512,1024]{1,0:T(8,128)(4,1)S(1)} %iota_compare_fusion.1) | copy-start | bytes 1572868
  16.7 170.2 %copy-start.5 = (pred[512,1024]{1,0:T(8,128)(4,1)}, pred[512,1024]{1,0:T(8,128)(4,1)S(1)}, u32[]{:S(2)}) copy-start(pred[512,1024]{1,0:T(8,128)(4,1)S(1)} %iota_compare_fusion) | copy-start | bytes 1572868
  171.9 15.0 %copy-start.31 = (f32[4,512]{1,0:T(4,128)}, f32[4,512]{1,0:T(4,128)S(1)}, u32[]{:S(2)}) copy-start(f32[4,512]{1,0:T(4,128)S(1)} %get-tuple-element.42) | copy-start | bytes 24580
  173.4 16.1 %copy-start.33 = (f32[4,512]{1,0:T(4,128)}, f32[4,512]{1,0:T(4,128)S(1)}, u32[]{:S(2)}) copy-start(f32[4,512]{1,0:T(4,128)S(1)} %get-tuple-element.44) | copy-start | bytes 24580
  177.6 9.3 copy-start.37
  179.9 9.5 copy-start.35
  181.5 5.4 copy-start.1
  181.5 8.0 slice-start.2
  192.4 26.3 %copy-start.26 = (bf16[1024,4,128]{0,2,1:T(8,128)(2,1)}, bf16[1024,4,128]{0,2,1:T(8,128)(2,1)S(1)}, u32[]{:S(2)}) copy-start(bf16[1024,4,128]{0,2,1:T(8,128)(2,1)S(1)} %pad_maximum_fusion.2) | copy-start | bytes 3145732
  218.7 144.7 %copy-start.3 = (bf16[1,256,2048]{2,1,0:T(8,128)(2,1)S(1)}, bf16[1,256,2048]{2,1,0:T(8,128)(2,1)}, u32[]{:S(2)}) copy-start(bf16[1,256,2048]{2,1,0:T(8,128)(2,1)} %param.10) | copy-start | bytes 3145732
  218.8 201.7 %all-gather.24.cloned.1.call-start = ((), (), s32[]{:S(2)}) async-start(), calls=%async_computation.18 | async-start | bytes 9437184 | tf_op jit(solution)/shard_map/all_gather | solution.py:82
  219.5 283.8 %all-gather.22.cloned.1.call-start = ((), (), s32[]{:S(2)}) async-start(), calls=%async_computation.17 | async-start | bytes 5242880 | tf_op jit(solution)/shard_map/all_gather | solution.py:143
  366.9 191.3 %all-gather.26.cloned.1.call-start = ((), (), s32[]{:S(2)}) async-start(), calls=%async_computation.19 | async-start | bytes 9437184 | tf_op jit(solution)/shard_map/all_gather | solution.py:83
  367.7 248.2 %all-gather.28.cloned.1.call-start = ((), (), s32[]{:S(2)}) async-start(), calls=%async_computation.20 | async-start | bytes 9437184 | tf_op jit(solution)/shard_map/all_gather | solution.py:85
  368.3 338.5 %reduce-scatter.14.cloned.1.call-start = ((), (), s32[]{:S(2)}) async-start(), calls=%async_computation.21 | async-start | bytes 5242880 | tf_op jit(solution)/shard_map/reduce_scatter | solution.py:149
  629.8 77.0 %copy-start.12 = (bf16[1,256,2048]{2,1,0:T(8,128)(2,1)S(1)}, bf16[1,256,2048]{2,1,0:T(8,128)(2,1)}, u32[]{:S(2)}) copy-start(bf16[1,256,2048]{2,1,0:T(8,128)(2,1)} %param.11) | copy-start | bytes 3145732
  629.8 161.1 %all-gather.30.cloned.1.call-start = ((), (), s32[]{:S(2)}) async-start(), calls=%async_computation.22 | async-start | bytes 5242880 | tf_op jit(solution)/shard_map/all_gather | solution.py:171
  709.5 203.4 %reduce-scatter.16.cloned.1.call-start = ((), (), s32[]{:S(2)}) async-start(), calls=%async_computation.23 | async-start | bytes 5242880 | tf_op jit(solution)/shard_map/reduce_scatter | solution.py:185
  811.6 12.7 copy-start.47
  837.4 163.6 %all-gather.32.cloned.1.call-start = ((), (), s32[]{:S(2)}) async-start(), calls=%async_computation.24 | async-start | bytes 5242880 | tf_op jit(solution)/shard_map/all_gather | solution.py:189
  919.7 209.8 %reduce-scatter.32.cloned.1.call-start = ((), (), s32[]{:S(2)}) async-start(), calls=%async_computation.32 | async-start | bytes 9437184 | tf_op jit(solution)/shard_map/reduce_scatter | solution.py:266
  933.9 216.0 %reduce-scatter.30.cloned.1.call-start = ((), (), s32[]{:S(2)}) async-start(), calls=%async_computation.31 | async-start | bytes 9437184 | tf_op jit(solution)/shard_map/reduce_scatter | solution.py:260
  948.5 276.0 %reduce-scatter.28.cloned.1.call-start = ((), (), s32[]{:S(2)}) async-start(), calls=%async_computation.30 | async-start | bytes 9437184 | tf_op jit(solution)/shard_map/reduce_scatter | solution.py:257
  962.6 38.5 %copy-start.46 = (bf16[512,2048]{1,0:T(8,128)(2,1)S(1)}, bf16[512,2048]{1,0:T(8,128)(2,1)}, u32[]{:S(2)}) copy-start(bf16[512,2048]{1,0:T(8,128)(2,1)} %all-gather.20.cloned.1.call-done) | copy-start | bytes 6291460
  962.6 306.5 %reduce-scatter.26.cloned.1.call-start = ((), (), s32[]{:S(2)}) async-start(), calls=%async_computation.29 | async-start | bytes 2359296 | tf_op jit(solution)/shard_map/reduce_scatter | solution.py:263
  1001.1 4.8 copy-start.27
  1001.1 4.8 copy-start.44
  1005.9 18.7 %copy-start.17 = (bf16[512,512]{0,1:T(8,128)(2,1)}, bf16[512,512]{0,1:T(8,128)(2,1)S(1)}, u32[]{:S(2)}) copy-start(bf16[512,512]{0,1:T(8,128)(2,1)S(1)} %get-tuple-element.37) | copy-start | bytes 1572868
  1009.6 304.1 %reduce-scatter.24.cloned.1.call-start = ((), (), s32[]{:S(2)}) async-start(), calls=%async_computation.28 | async-start | bytes 2359296 | tf_op jit(solution)/shard_map/reduce_scatter | solution.py:254
  1009.9 14.7 slice-start
  1016.9 5.3 copy-start.11
  1016.9 7.6 slice-start.1
  1022.3 4.7 copy-start.9
  1035.4 8.2 copy-start.14
  1043.4 315.1 %reduce-scatter.20.cloned.1.call-start = ((), (), s32[]{:S(2)}) async-start(), calls=%async_computation.26 | async-start | bytes 2359296 | tf_op jit(solution)/shard_map/reduce_scatter | solution.py:248
  1067.2 335.8 %reduce-scatter.22.cloned.1.call-start = ((), (), s32[]{:S(2)}) async-start(), calls=%async_computation.27 | async-start | bytes 2359296 | tf_op jit(solution)/shard_map/reduce_scatter | solution.py:251
  1068.6 6.4 copy-start.29
  1075.0 407.2 %reduce-scatter.18.cloned.1.call-start = ((), (), s32[]{:S(2)}) async-start(), calls=%async_computation.25 | async-start | bytes 5242880 | tf_op jit(solution)/shard_map/reduce_scatter | solution.py:243
  1132.2 350.0 %copy-start.4 = (bf16[1,256,2048]{2,1,0:T(8,128)(2,1)S(1)}, bf16[1,256,2048]{2,1,0:T(8,128)(2,1)}, u32[]{:S(2)}) copy-start(bf16[1,256,2048]{2,1,0:T(8,128)(2,1)} %param.10) | copy-start | bytes 3145732
  1132.2 350.0 %copy-start.40 = (f32[256]{0:T(256)S(1)}, f32[256]{0:T(256)}, u32[]{:S(2)}) copy-start(f32[256]{0:T(256)} %copy-done.39) | copy-start | bytes 3076
  1132.2 350.0 %copy-start.42 = (f32[256]{0:T(256)S(1)}, f32[256]{0:T(256)}, u32[]{:S(2)}) copy-start(f32[256]{0:T(256)} %copy-done.41) | copy-start | bytes 3076
  1152.6 331.5 %copy-start.16 = (f32[256,2048]{1,0:T(8,128)S(1)}, f32[256,2048]{1,0:T(8,128)}, u32[]{:S(2)}) copy-start(f32[256,2048]{1,0:T(8,128)} %get-tuple-element.16) | copy-start | bytes 6291460
  (28 other events, 72.1 us)
Sparse Core Ops, SparseCore 0:
  9.9 30.6 all-gather.17
  42.7 80.7 all-gather.11
  125.4 26.4 all-gather.15
  153.6 27.8 all-gather.13
  183.2 28.2 all-gather.19
  218.9 144.4 reduce-scatter.11
  365.3 55.0 all-gather.23
  422.6 80.7 all-gather.21
  505.2 52.9 all-gather.25
  559.9 55.9 all-gather.27
  629.9 76.7 reduce-scatter.13
  709.6 81.2 all-gather.29
  837.6 75.2 reduce-scatter.15
  919.8 81.2 all-gather.31
  1004.4 69.7 reduce-scatter.31
  1077.9 71.8 reduce-scatter.29
  1153.1 71.2 reduce-scatter.27
  1227.9 41.1 reduce-scatter.25
  1272.4 41.2 reduce-scatter.23
  1317.2 41.2 reduce-scatter.19
  1361.7 41.2 reduce-scatter.21
  1405.4 76.7 reduce-scatter.17
where the time goes:
time: 1510 us; the launch traced here: 1500 us
  waiting for transfers between devices  1100 us (73%)
  matrix products  233 us (15%)
  other arithmetic  67.9 us (4%)
  blocking collectives  53.5 us (4%)
  local copies, waits for them, and re-layouts  21.9 us (1%)
  between operations  19.5 us (1%)
    reduce_scatter x1, waiting for transfers between devices, local(): lax.psum_scatter(jnp.dot(attended, out_full, preferred_element_type=jnp.f...  144 us
    all_gather x1, waiting for transfers between devices, local(): features_two = lax.all_gather(normed_two, 'tensor', axis=0, tiled=True)  82.9 us
    all_gather x1, waiting for transfers between devices, local(): features = lax.all_gather(normed, 'tensor', axis=0, tiled=True)  82.9 us
    all_gather x1, waiting for transfers between devices, local(): lax.all_gather(grad_result.astype(jnp.bfloat16), 'tensor', axis=0, tiled=...  81.4 us
    reduce_scatter x1, waiting for transfers between devices, local(): lax.psum_scatter(features_grad.astype(jnp.bfloat16), 'tensor', scatter_di...  77.4 us
    reduce_scatter x1, waiting for transfers between devices, local(): lax.psum_scatter(feature_grad.astype(jnp.bfloat16), 'tensor', scatter_dim...  75.4 us
    reduce_scatter x1, waiting for transfers between devices, local(): lax.psum_scatter(grad_gate.astype(jnp.bfloat16), 'dp', scatter_dimension=...  71.8 us
    reduce_scatter x1, waiting for transfers between devices, local(): lax.psum_scatter(jnp.dot(hidden, down_full, preferred_element_type=jnp.fl...  61.4 us
  transfers between devices with their start and end apart: 22, of which 21 were waited for; matrix products, arithmetic and copies ran while one was open for 16% of the time, Pallas kernels for 0%

commit v1 on v0

--- a/solution.py
+++ b/solution.py
@@ -140,7 +140,14 @@
     )
     residual = rows_in + attn_out
     normed_two = layer_norm(residual).astype(jnp.bfloat16)
-    features_two = lax.all_gather(normed_two, "tensor", axis=0, tiled=True)
+    ring = [normed_two]
+    for hop in range(3):
+        ring.append(lax.ppermute(ring[-1], "tensor", [(dev, (dev + 1) % 4) for dev in range(4)]))
+    features_two = jnp.roll(
+        jnp.concatenate(ring[::-1], axis=0),
+        (lax.axis_index("tensor") + 1) * ring[0].shape[0],
+        axis=0,
+    )
     gate_pre = jnp.dot(features_two, gate_full, preferred_element_type=jnp.float32)
     up_pre = jnp.dot(features_two, up_full, preferred_element_type=jnp.float32)
     gate_sigmoid = jax.nn.sigmoid(gate_pre)

time: 1510 us -> 1430 us (0.947)
  waiting for transfers between devices: 1100 us -> 1000 us
    all_gather x1 -> x0, waiting for transfers between devices: 82.9 us -> none  [local(): features_two = lax.all_gather(normed_two, 'tensor', axis=0, tiled=True)]
    ppermute x0 -> x3, waiting for transfers between devices: none -> 76.1 us  [local(): lax.ppermute(ring[-1], 'tensor', [(dev, (dev + 1) % 4) for dev in range(4)])]
    all_gather x1, waiting for transfers between devices: 52.1 us -> 0.01 us  [local(): lax.all_gather(w_gate, 'dp', axis=0, tiled=True)]
    all_gather x1, waiting for transfers between devices: 40 us -> 4.32 us  [local(): lax.all_gather(w_up, 'dp', axis=0, tiled=True)]
  transfers between devices with their start and end apart: 22 -> 24, of which waited for: 21 -> 22; matrix products, arithmetic and copies ran while one was open for 16% -> 18% of each run, Pallas kernels for 0% -> 0%
where the time goes in v1:
time: 1430 us; the launch traced here: 1410 us
  waiting for transfers between devices  1000 us (70%)
  matrix products  233 us (16%)
  other arithmetic  69.4 us (5%)
  blocking collectives  53.3 us (4%)
  local copies, waits for them, and re-layouts  33.7 us (2%)
  between operations  19.4 us (1%)
    reduce_scatter x1, waiting for transfers between devices, local(): lax.psum_scatter(jnp.dot(attended, out_full, preferred_element_type=jnp.f...  142 us
    all_gather x1, waiting for transfers between devices, local(): features = lax.all_gather(normed, 'tensor', axis=0, tiled=True)  82.9 us
    all_gather x1, waiting for transfers between devices, local(): lax.all_gather(grad_result.astype(jnp.bfloat16), 'tensor', axis=0, tiled=...  81.4 us
    reduce_scatter x1, waiting for transfers between devices, local(): lax.psum_scatter(features_grad.astype(jnp.bfloat16), 'tensor', scatter_di...  77.4 us
    ppermute x3, waiting for transfers between devices, local(): lax.ppermute(ring[-1], 'tensor', [(dev, (dev + 1) % 4) for dev in range(4)])  76.1 us
    reduce_scatter x1, waiting for transfers between devices, local(): lax.psum_scatter(feature_grad.astype(jnp.bfloat16), 'tensor', scatter_dim...  75.4 us
    reduce_scatter x1, waiting for transfers between devices, local(): lax.psum_scatter(grad_gate.astype(jnp.bfloat16), 'dp', scatter_dimension=...  71.8 us
    reduce_scatter x1, waiting for transfers between devices, local(): lax.psum_scatter(jnp.dot(hidden, down_full, preferred_element_type=jnp.fl...  61.4 us
  transfers between devices with their start and end apart: 24, of which 22 were waited for; matrix products, arithmetic and copies ran while one was open for 18% of the time, Pallas kernels for 0%

profile of v1, /device:TPU:0, one launch (start us, length us, event | category | flops | bytes accessed | tf_op | source)
XLA Modules:
  0.0 1414.6 jit_solution(12315345629122144650)
XLA Ops:
  19.6 21.0 %all-gather.17.cloned.1.call-done = bf16[2048,512]{1,0:T(8,128)(2,1)} async-done(((bf16[256,512]{1,0:T(8,128)(2,1)}), bf16[2048,512]{1,0:T(8,128)(2,1)}) %all-gather.17.cloned.1.call-update) | async-done | bytes 2097168 | tf_op jit(solution)/shard_map/all_gather | solution.py:80
  40.5 82.9 %all-gather.11.cloned.1.call-done = bf16[1024,2048]{1,0:T(8,128)(2,1)} async-done(((bf16[256,2048]{1,0:T(8,128)(2,1)}), bf16[1024,2048]{1,0:T(8,128)(2,1)}) %all-gather.11.cloned.1.call-update) | async-done | bytes 4194320 | tf_op jit(solution)/shard_map/all_gather | solution.py:96
  123.5 5.2 fusion.76
  135.3 16.5 %all-gather.15.cloned.1.call-done = bf16[2048,512]{1,0:T(8,128)(2,1)} async-done(((bf16[256,512]{1,0:T(8,128)(2,1)}), bf16[2048,512]{1,0:T(8,128)(2,1)}) %all-gather.15.cloned.1.call-update) | async-done | bytes 2097168 | tf_op jit(solution)/shard_map/all_gather | solution.py:79
  151.8 5.2 fusion.75
  164.9 4.3 multiply_subtract_fusion.1
  181.5 5.4 convolution_convert_fusion.9
  192.4 19.1 %all-gather.19.cloned.1.call-done = bf16[512,2048]{1,0:T(8,128)(2,1)} async-done(((bf16[512,256]{1,0:T(8,128)(2,1)}), bf16[512,2048]{1,0:T(8,128)(2,1)}) %all-gather.19.cloned.1.call-update) | async-done | bytes 2097168 | tf_op jit(solution)/shard_map/all_gather | solution.py:84
  211.5 7.2 fusion.77
  221.0 142.3 %reduce-scatter.12.cloned.1.call-done = f32[256,2048]{1,0:T(8,128)} async-done(((f32[1024,2048]{1,0:T(8,128)}), f32[256,2048]{1,0:T(8,128)}) %reduce-scatter.12.cloned.1.call-update) | async-done | bytes 2097168 | tf_op jit(solution)/shard_map/reduce_scatter | solution.py:135
  367.2 25.3 %collective-permute-done = bf16[256,2048]{1,0:T(8,128)(2,1)S(1)} collective-permute-done((bf16[256,2048]{1,0:T(8,128)(2,1)S(1)}, bf16[256,2048]{1,0:T(8,128)(2,1)S(1)}, u32[]{:S(2)}, u32[]{:S(2)}) %collective-permute-start) | collective-permute-done | bytes 1048608 | tf_op jit(solution)/shard_map/ppermute | solution.py:145
  392.5 25.7 %collective-permute-done.1 = bf16[256,2048]{1,0:T(8,128)(2,1)} collective-permute-done((bf16[256,2048]{1,0:T(8,128)(2,1)S(1)}, bf16[256,2048]{1,0:T(8,128)(2,1)}, u32[]{:S(2)}, u32[]{:S(2)}) %collective-permute-start.1) | collective-permute-done | bytes 1048608 | tf_op jit(solution)/shard_map/ppermute | solution.py:145
  418.3 25.0 %collective-permute-done.2 = bf16[256,2048]{1,0:T(8,128)(2,1)} collective-permute-done((bf16[256,2048]{1,0:T(8,128)(2,1)}, bf16[256,2048]{1,0:T(8,128)(2,1)}, u32[]{:S(2)}, u32[]{:S(2)}) %collective-permute-start.2) | collective-permute-done | bytes 1048608 | tf_op jit(solution)/shard_map/ppermute | solution.py:145
  457.6 14.8 %fusion.21 = f32[1024,2048]{1,0:T(8,128)} fusion(bf16[2048,2048]{1,0:T(8,128)(2,1)} %all-gather.21.cloned.1.call-done, bf16[2048,2048]{1,0:T(8,128)(2,1)} %constant_dynamic-update-slice_fusion, s32[]{:T(128)S(6)} %select_n.29), kind=kOutput, calls=%fused_computation.51 | convolution fusion | flops 8589934592 | bytes 20971524 | tf_op jit(solution)/shard_map/dot_general | solution.py:151
  472.4 4.3 all-gather.23.cloned.1.call-done
  476.7 17.3 %multiply_convert_fusion.4 = (bf16[1024,2048]{1,0:T(8,128)(2,1)}, f32[1024,2048]{1,0:T(8,128)}) fusion(f32[1024,2048]{1,0:T(8,128)} %fusion.21, bf16[2048,2048]{1,0:T(8,128)(2,1)} %all-gather.23.cloned.1.call-done, bf16[2048,2048]{1,0:T(8,128)(2,1)} %constant_dynamic-update-slice_fusion, s32[]{:T(128)S(6)} %select_n.29), kind=kOutput, calls=%fused_computation.10 | convolution fusion | flops 8602517504 | bytes 33554436 | tf_op jit(solution)/shard_map/dot_general | solution.py:152
  494.0 40.6 %all-gather.25.cloned.1.call-done = bf16[2048,2048]{1,0:T(8,128)(2,1)} async-done(((bf16[2048,256]{1,0:T(8,128)(2,1)}), bf16[2048,2048]{1,0:T(8,128)(2,1)}) %all-gather.25.cloned.1.call-update) | async-done | bytes 8388624 | tf_op jit(solution)/shard_map/all_gather | solution.py:85
  534.6 13.9 convolution_convert_fusion.3
  549.3 14.0 psum.15
  564.0 61.4 %reduce-scatter.14.cloned.1.call-done = bf16[256,2048]{1,0:T(8,128)(2,1)} async-done(((bf16[1024,2048]{1,0:T(8,128)(2,1)}), bf16[256,2048]{1,0:T(8,128)(2,1)}) %reduce-scatter.14.cloned.1.call-update) | async-done | bytes 1048592 | tf_op jit(solution)/shard_map/reduce_scatter | solution.py:156
  628.2 81.4 %all-gather.27.cloned.1.call-done = bf16[1024,2048]{1,0:T(8,128)(2,1)} async-done(((bf16[256,2048]{1,0:T(8,128)(2,1)}), bf16[1024,2048]{1,0:T(8,128)(2,1)}) %all-gather.27.cloned.1.call-update) | async-done | bytes 4194320 | tf_op jit(solution)/shard_map/all_gather | solution.py:178
  709.6 20.8 %multiply_convert_fusion.2 = (bf16[1024,2048]{1,0:T(8,128)(2,1)}, bf16[1024,2048]{1,0:T(8,128)(2,1)}) fusion(f32[1024,2048]{1,0:T(8,128)} %fusion.21, f32[1024,2048]{1,0:T(8,128)} %get-tuple-element.47, bf16[1024,2048]{1,0:T(8,128)(2,1)} %all-gather.27.cloned.1.call-done, bf16[2048,2048]{1,0:T(8,128)(2,1)} %all-gather.25.cloned.1.call-done), kind=kOutput, calls=%fused_computation.8 | convolution fusion | flops 8617197568 | bytes 37748736 | tf_op jit(solution)/shard_map/td,fd->tf/dot_general | solution.py:180
  730.4 12.7 fusion.78
  743.1 13.1 add_convert_fusion.1
  756.2 75.4 %reduce-scatter.16.cloned.1.call-done = bf16[256,2048]{1,0:T(8,128)(2,1)} async-done(((bf16[1024,2048]{1,0:T(8,128)(2,1)}), bf16[256,2048]{1,0:T(8,128)(2,1)}) %reduce-scatter.16.cloned.1.call-update) | async-done | bytes 1048592 | tf_op jit(solution)/shard_map/reduce_scatter | solution.py:192
  838.5 14.1 convolution_convert_fusion
  852.7 14.2 %convolution_convert_fusion.1 = bf16[2048,2048]{1,0:T(8,128)(2,1)} fusion(bf16[1024,2048]{1,0:T(8,128)(2,1)} %get-tuple-element.19, bf16[2048,2048]{1,0:T(8,128)(2,1)} %constant_dynamic-update-slice_fusion, s32[]{:T(128)S(6)} %select_n.29), kind=kOutput, calls=%fused_computation.18 | convolution fusion | flops 8594128896 | bytes 16777220 | tf_op jit(solution)/shard_map/td,tf->df/dot_general | solution.py:188
  867.0 14.0 convolution_convert_fusion.2
  881.7 38.1 %all-gather.29.cloned.1.call-done = bf16[1024,2048]{1,0:T(8,128)(2,1)} async-done(((bf16[256,2048]{1,0:T(8,128)(2,1)}), bf16[1024,2048]{1,0:T(8,128)(2,1)}) %all-gather.29.cloned.1.call-update) | async-done | bytes 4194320 | tf_op jit(solution)/shard_map/all_gather | solution.py:196
  919.9 4.7 convolution_convert_fusion.8
  928.9 6.9 multiply_reduce_fusion.1
  935.9 5.3 multiply_convert_fusion.1
  950.6 3.9 convolution_convert_fusion.5
  954.4 7.9 multiply_reduce_fusion
  962.6 3.8 fusion.56
  966.4 7.1 multiply_convert_fusion
  980.0 6.2 convolution_convert_fusion.7
  987.6 6.3 convolution_convert_fusion.6
  994.1 4.5 fusion.80
  1001.0 6.7 add_convert_fusion
  1008.3 39.2 %psum.14 = f32[]{:T(128)} all-reduce(f32[]{:T(128)} %get-tuple-element.11), channel_id=1, replica_groups=mesh['dp'=8,'tensor'=4] {'dp','tensor'}, use_global_device_ids=true, to_apply=%region_11.12 | all-reduce | flops 1 | bytes 8 | tf_op jit(solution)/shard_map/psum | solution.py:165
  1051.0 17.7 %reduce-scatter.30.cloned.1.call-done = bf16[256,2048]{1,0:T(8,128)(2,1)} async-done(((bf16[2048,2048]{1,0:T(8,128)(2,1)}), bf16[256,2048]{1,0:T(8,128)(2,1)}) %reduce-scatter.30.cloned.1.call-update) | async-done | bytes 1048592 | tf_op jit(solution)/shard_map/reduce_scatter | solution.py:267
  1071.4 71.8 %reduce-scatter.28.cloned.1.call-done = bf16[256,2048]{1,0:T(8,128)(2,1)} async-done(((bf16[2048,2048]{1,0:T(8,128)(2,1)}), bf16[256,2048]{1,0:T(8,128)(2,1)}) %reduce-scatter.28.cloned.1.call-update) | async-done | bytes 1048592 | tf_op jit(solution)/shard_map/reduce_scatter | solution.py:264
  1146.0 42.0 %reduce-scatter.26.cloned.1.call-done = bf16[512,256]{1,0:T(8,128)(2,1)} async-done(((bf16[512,2048]{1,0:T(8,128)(2,1)}), bf16[512,256]{1,0:T(8,128)(2,1)}) %reduce-scatter.26.cloned.1.call-update) | async-done | bytes 262160 | tf_op jit(solution)/shard_map/reduce_scatter | solution.py:270
  1189.8 42.6 %reduce-scatter.24.cloned.1.call-done = bf16[256,512]{1,0:T(8,128)(2,1)} async-done(((bf16[2048,512]{1,0:T(8,128)(2,1)}), bf16[256,512]{1,0:T(8,128)(2,1)}) %reduce-scatter.24.cloned.1.call-update) | async-done | bytes 262160 | tf_op jit(solution)/shard_map/reduce_scatter | solution.py:261
  1234.2 43.1 %reduce-scatter.20.cloned.1.call-done = bf16[256,512]{1,0:T(8,128)(2,1)} async-done(((bf16[2048,512]{1,0:T(8,128)(2,1)}), bf16[256,512]{1,0:T(8,128)(2,1)}) %reduce-scatter.20.cloned.1.call-update) | async-done | bytes 262160 | tf_op jit(solution)/shard_map/reduce_scatter | solution.py:255
  1279.1 42.6 %reduce-scatter.22.cloned.1.call-done = bf16[256,512]{1,0:T(8,128)(2,1)} async-done(((bf16[2048,512]{1,0:T(8,128)(2,1)}), bf16[256,512]{1,0:T(8,128)(2,1)}) %reduce-scatter.22.cloned.1.call-update) | async-done | bytes 262160 | tf_op jit(solution)/shard_map/reduce_scatter | solution.py:258
  1323.5 77.4 %reduce-scatter.18.cloned.1.call-done = bf16[256,2048]{1,0:T(8,128)(2,1)} async-done(((bf16[1024,2048]{1,0:T(8,128)(2,1)}), bf16[256,2048]{1,0:T(8,128)(2,1)}) %reduce-scatter.18.cloned.1.call-update) | async-done | bytes 1048592 | tf_op jit(solution)/shard_map/reduce_scatter | solution.py:250
  (228 shorter events, 119.9 us)
Async XLA Ops:
  7.2 33.4 %all-gather.17.cloned.1.call-start = ((), (), s32[]{:S(2)}) async-start(), calls=%async_computation.14 | async-start | bytes 2359296 | tf_op jit(solution)/shard_map/all_gather | solution.py:80
  7.9 115.6 %all-gather.11.cloned.1.call-start = ((), (), s32[]{:S(2)}) async-start(), calls=%async_computation.11 | async-start | bytes 5242880 | tf_op jit(solution)/shard_map/all_gather | solution.py:96
  14.2 137.6 %all-gather.15.cloned.1.call-start = ((), (), s32[]{:S(2)}) async-start(), calls=%async_computation.13 | async-start | bytes 2359296 | tf_op jit(solution)/shard_map/all_gather | solution.py:79
  14.9 166.6 %all-gather.13.cloned.1.call-start = ((), (), s32[]{:S(2)}) async-start(), calls=%async_computation.12 | async-start | bytes 2359296 | tf_op jit(solution)/shard_map/all_gather | solution.py:81
  15.5 196.0 %all-gather.19.cloned.1.call-start = ((), (), s32[]{:S(2)}) async-start(), calls=%async_computation.15 | async-start | bytes 2359296 | tf_op jit(solution)/shard_map/all_gather | solution.py:84
  16.1 347.3 %reduce-scatter.12.cloned.1.call-start = ((), (), s32[]{:S(2)}) async-start(), calls=%async_computation.16 | async-start | bytes 10485760 | tf_op jit(solution)/shard_map/reduce_scatter | solution.py:135
  16.3 173.1 %copy-start.7 = (pred[512,1024]{1,0:T(8,128)(4,1)}, pred[512,1024]{1,0:T(8,128)(4,1)S(1)}, u32[]{:S(2)}) copy-start(pred[512,1024]{1,0:T(8,128)(4,1)S(1)} %iota_compare_fusion.1) | copy-start | bytes 1572868
  16.7 170.2 %copy-start.5 = (pred[512,1024]{1,0:T(8,128)(4,1)}, pred[512,1024]{1,0:T(8,128)(4,1)S(1)}, u32[]{:S(2)}) copy-start(pred[512,1024]{1,0:T(8,128)(4,1)S(1)} %iota_compare_fusion) | copy-start | bytes 1572868
  171.9 15.0 %copy-start.31 = (f32[4,512]{1,0:T(4,128)}, f32[4,512]{1,0:T(4,128)S(1)}, u32[]{:S(2)}) copy-start(f32[4,512]{1,0:T(4,128)S(1)} %get-tuple-element.42) | copy-start | bytes 24580
  173.4 16.1 %copy-start.33 = (f32[4,512]{1,0:T(4,128)}, f32[4,512]{1,0:T(4,128)S(1)}, u32[]{:S(2)}) copy-start(f32[4,512]{1,0:T(4,128)S(1)} %get-tuple-element.44) | copy-start | bytes 24580
  177.5 9.4 copy-start.37
  179.9 9.5 copy-start.35
  181.5 5.4 copy-start.1
  181.5 8.0 slice-start.2
  192.4 26.3 %copy-start.26 = (bf16[1024,4,128]{0,2,1:T(8,128)(2,1)}, bf16[1024,4,128]{0,2,1:T(8,128)(2,1)S(1)}, u32[]{:S(2)}) copy-start(bf16[1024,4,128]{0,2,1:T(8,128)(2,1)S(1)} %pad_maximum_fusion.2) | copy-start | bytes 3145732
  218.7 144.7 %copy-start.3 = (bf16[1,256,2048]{2,1,0:T(8,128)(2,1)S(1)}, bf16[1,256,2048]{2,1,0:T(8,128)(2,1)}, u32[]{:S(2)}) copy-start(bf16[1,256,2048]{2,1,0:T(8,128)(2,1)} %param.10) | copy-start | bytes 3145732
  218.8 238.9 %all-gather.21.cloned.1.call-start = ((), (), s32[]{:S(2)}) async-start(), calls=%async_computation.17 | async-start | bytes 9437184 | tf_op jit(solution)/shard_map/all_gather | solution.py:82
  219.5 257.2 %all-gather.23.cloned.1.call-start = ((), (), s32[]{:S(2)}) async-start(), calls=%async_computation.18 | async-start | bytes 9437184 | tf_op jit(solution)/shard_map/all_gather | solution.py:83
  220.3 314.3 %all-gather.25.cloned.1.call-start = ((), (), s32[]{:S(2)}) async-start(), calls=%async_computation.19 | async-start | bytes 9437184 | tf_op jit(solution)/shard_map/all_gather | solution.py:85
  221.0 404.4 %reduce-scatter.14.cloned.1.call-start = ((), (), s32[]{:S(2)}) async-start(), calls=%async_computation.20 | async-start | bytes 5242880 | tf_op jit(solution)/shard_map/reduce_scatter | solution.py:156
  365.9 26.6 %collective-permute-start = (bf16[256,2048]{1,0:T(8,128)(2,1)S(1)}, bf16[256,2048]{1,0:T(8,128)(2,1)S(1)}, u32[]{:S(2)}, u32[]{:S(2)}) collective-permute-start(bf16[256,2048]{1,0:T(8,128)(2,1)S(1)} %fusion.42), channel_id=1, source_target_pairs={{0,1},{1,2},{2,3},{3,0},{4,5},{5,6},{6,7},{7,4},{8,9},{9,10},{10,1... | collective-permute-start | bytes 3145736 | tf_op jit(solution)/shard_map/ppermute | solution.py:145
  392.5 25.7 %collective-permute-start.1 = (bf16[256,2048]{1,0:T(8,128)(2,1)S(1)}, bf16[256,2048]{1,0:T(8,128)(2,1)}, u32[]{:S(2)}, u32[]{:S(2)}) collective-permute-start(bf16[256,2048]{1,0:T(8,128)(2,1)S(1)} %collective-permute-done), channel_id=1, source_target_pairs={{0,1},{1,2},{2,3},{3,0},{4,5},{5,6},{6,7},{7,4},{8,9},{9,10},{10,1... | collective-permute-start | bytes 3145736 | tf_op jit(solution)/shard_map/ppermute | solution.py:145
  418.3 25.0 %collective-permute-start.2 = (bf16[256,2048]{1,0:T(8,128)(2,1)}, bf16[256,2048]{1,0:T(8,128)(2,1)}, u32[]{:S(2)}, u32[]{:S(2)}) collective-permute-start(bf16[256,2048]{1,0:T(8,128)(2,1)} %collective-permute-done.1), channel_id=1, source_target_pairs={{0,1},{1,2},{2,3},{3,0},{4,5},{5,6},{6,7},{7,4},{8,9},{9,10},{10,1... | collective-permute-start | bytes 3145736 | tf_op jit(solution)/shard_map/ppermute | solution.py:145
  548.5 77.0 %copy-start.12 = (bf16[1,256,2048]{2,1,0:T(8,128)(2,1)S(1)}, bf16[1,256,2048]{2,1,0:T(8,128)(2,1)}, u32[]{:S(2)}) copy-start(bf16[1,256,2048]{2,1,0:T(8,128)(2,1)} %param.11) | copy-start | bytes 3145732
  548.5 161.1 %all-gather.27.cloned.1.call-start = ((), (), s32[]{:S(2)}) async-start(), calls=%async_computation.21 | async-start | bytes 5242880 | tf_op jit(solution)/shard_map/all_gather | solution.py:178
  628.2 203.5 %reduce-scatter.16.cloned.1.call-start = ((), (), s32[]{:S(2)}) async-start(), calls=%async_computation.22 | async-start | bytes 5242880 | tf_op jit(solution)/shard_map/reduce_scatter | solution.py:192
  730.4 12.7 copy-start.47
  756.2 163.7 %all-gather.29.cloned.1.call-start = ((), (), s32[]{:S(2)}) async-start(), calls=%async_computation.23 | async-start | bytes 5242880 | tf_op jit(solution)/shard_map/all_gather | solution.py:196
  838.5 209.8 %reduce-scatter.32.cloned.1.call-start = ((), (), s32[]{:S(2)}) async-start(), calls=%async_computation.31 | async-start | bytes 9437184 | tf_op jit(solution)/shard_map/reduce_scatter | solution.py:273
  852.7 216.0 %reduce-scatter.30.cloned.1.call-start = ((), (), s32[]{:S(2)}) async-start(), calls=%async_computation.30 | async-start | bytes 9437184 | tf_op jit(solution)/shard_map/reduce_scatter | solution.py:267
  866.9 276.3 %reduce-scatter.28.cloned.1.call-start = ((), (), s32[]{:S(2)}) async-start(), calls=%async_computation.29 | async-start | bytes 9437184 | tf_op jit(solution)/shard_map/reduce_scatter | solution.py:264
  881.0 38.9 %copy-start.46 = (bf16[512,2048]{1,0:T(8,128)(2,1)S(1)}, bf16[512,2048]{1,0:T(8,128)(2,1)}, u32[]{:S(2)}) copy-start(bf16[512,2048]{1,0:T(8,128)(2,1)} %all-gather.19.cloned.1.call-done) | copy-start | bytes 6291460
  881.0 307.0 %reduce-scatter.26.cloned.1.call-start = ((), (), s32[]{:S(2)}) async-start(), calls=%async_computation.28 | async-start | bytes 2359296 | tf_op jit(solution)/shard_map/reduce_scatter | solution.py:270
  919.9 4.8 copy-start.44
  924.7 18.8 %copy-start.17 = (bf16[512,512]{0,1:T(8,128)(2,1)}, bf16[512,512]{0,1:T(8,128)(2,1)S(1)}, u32[]{:S(2)}) copy-start(bf16[512,512]{0,1:T(8,128)(2,1)S(1)} %get-tuple-element.37) | copy-start | bytes 1572868
  928.5 303.9 %reduce-scatter.24.cloned.1.call-start = ((), (), s32[]{:S(2)}) async-start(), calls=%async_computation.27 | async-start | bytes 2359296 | tf_op jit(solution)/shard_map/reduce_scatter | solution.py:261
  928.9 14.5 %slice-start = ((s8[8388608]{0:T(1024)(128)(4,1)}), s8[4194304]{0:T(1024)(128)(4,1)S(1)}, s32[]{:S(2)}) async-start(s8[8388608]{0:T(1024)(128)(4,1)} %bitcast.121), calls=%async_computation.32 | async-start | bytes 8388608
  935.9 5.3 copy-start.11
  935.9 7.6 slice-start.1
  954.4 8.2 copy-start.14
  962.4 314.9 %reduce-scatter.20.cloned.1.call-start = ((), (), s32[]{:S(2)}) async-start(), calls=%async_computation.25 | async-start | bytes 2359296 | tf_op jit(solution)/shard_map/reduce_scatter | solution.py:255
  986.2 335.5 %reduce-scatter.22.cloned.1.call-start = ((), (), s32[]{:S(2)}) async-start(), calls=%async_computation.26 | async-start | bytes 2359296 | tf_op jit(solution)/shard_map/reduce_scatter | solution.py:258
  987.6 6.4 copy-start.29
  994.0 406.9 %reduce-scatter.18.cloned.1.call-start = ((), (), s32[]{:S(2)}) async-start(), calls=%async_computation.24 | async-start | bytes 5242880 | tf_op jit(solution)/shard_map/reduce_scatter | solution.py:250
  1051.0 349.9 %copy-start.4 = (bf16[1,256,2048]{2,1,0:T(8,128)(2,1)S(1)}, bf16[1,256,2048]{2,1,0:T(8,128)(2,1)}, u32[]{:S(2)}) copy-start(bf16[1,256,2048]{2,1,0:T(8,128)(2,1)} %param.10) | copy-start | bytes 3145732
  1051.0 349.9 %copy-start.40 = (f32[256]{0:T(256)S(1)}, f32[256]{0:T(256)}, u32[]{:S(2)}) copy-start(f32[256]{0:T(256)} %copy-done.39) | copy-start | bytes 3076
  1051.0 349.9 %copy-start.42 = (f32[256]{0:T(256)S(1)}, f32[256]{0:T(256)}, u32[]{:S(2)}) copy-start(f32[256]{0:T(256)} %copy-done.41) | copy-start | bytes 3076
  1071.4 331.4 %copy-start.16 = (f32[256,2048]{1,0:T(8,128)S(1)}, f32[256,2048]{1,0:T(8,128)}, u32[]{:S(2)}) copy-start(f32[256,2048]{1,0:T(8,128)} %get-tuple-element.16) | copy-start | bytes 6291460
  (30 other events, 82.2 us)
Sparse Core Ops, SparseCore 0:
  9.9 30.5 all-gather.16
  42.7 80.7 all-gather.10
  125.4 26.4 all-gather.14
  153.6 27.8 all-gather.12
  183.2 28.2 all-gather.18
  218.9 144.4 reduce-scatter.11
  365.3 55.0 all-gather.20
  422.3 54.3 all-gather.22
  478.6 55.9 all-gather.24
  548.6 76.7 reduce-scatter.13
  628.3 81.2 all-gather.26
  756.3 75.2 reduce-scatter.15
  838.6 81.2 all-gather.28
  923.2 69.8 reduce-scatter.31
  996.7 71.8 reduce-scatter.29
  1072.0 71.2 reduce-scatter.27
  1146.7 41.2 reduce-scatter.25
  1191.1 41.2 reduce-scatter.23
  1236.0 41.2 reduce-scatter.19
  1280.4 41.1 reduce-scatter.21
  1324.1 76.7 reduce-scatter.17
